TPU v7x, 32 devices: a whole 2x2x4 slice. The times are simulated.
32 devices in a mesh: seq: 8 (over y, x, core), exp: 4 (over z).
Axes of the slice: x: 2, y: 2, z: 4, core: 2. Of those that a mesh axis runs over, the one named last changes fastest.
Arguments:
- layer_input: bfloat16 [4, 4096, 768], P('exp', 'seq'), may hold values from -6 to 6
- token_ids: int32 [4, 4096], P('exp', 'seq'), may hold values from 0 to 8007, as said below
- segment_ids: int32 [4, 4096], P('exp'), may hold values from 0 to 7, never falling along the last dimension, each value on 1 to 1024 neighbouring positions
- hash_table: int32 [8008], replicated, may hold values from 0 to 3, as said below
- first_gain: float32 [768], replicated, may hold values from 0.25 to 1.75
- first_bias: float32 [768], replicated, may hold values from -1.5 to 1.5
- second_gain: float32 [768], replicated, may hold values from 0.25 to 1.75
- second_bias: float32 [768], replicated, may hold values from -1.5 to 1.5
- w_qkv: bfloat16 [768, 2304], replicated, may hold values from -0.21875 to 0.21875
- w_out: bfloat16 [768, 768], replicated, may hold values from -3 to 3
- w_up: bfloat16 [4, 768, 3072], P('exp'), may hold values from -0.21875 to 0.21875
- w_down: bfloat16 [4, 3072, 768], P('exp'), may hold values from -0.109375 to 0.109375
- cotangent: bfloat16 [4, 4096, 768], P('exp', 'seq'), may hold values from -6 to 6
Outputs:
- layer_output: bfloat16 [4, 4096, 768], P('exp', 'seq')
- grad_input: float32 [4, 4096, 768], P('exp', 'seq')
- grad_w_qkv: float32 [768, 2304], replicated
- grad_w_out: float32 [768, 768], replicated
- grad_first_gain: float32 [768], replicated
- grad_first_bias: float32 [768], replicated
- grad_second_gain: float32 [768], replicated
- grad_second_bias: float32 [768], replicated
- grad_w_up: float32 [4, 768, 3072], P('exp')
- grad_w_down: float32 [4, 3072, 768], P('exp')
Inputs may be any that keep to these rules, and one draw needn't show every extreme that they name: `token_ids`: token ids range over the vocabulary. Among the 512 positions that one device holds, hash_table sends exactly 256 to one expert, the same expert on all devices that hold the same positions of their sequences, and the other experts' counts differ from one another by at most one. `hash_table`: every expert is named by 2002 token ids. `segment_ids`: numbers never fall along a sequence; each document holds 1 to 1024 neighbouring positions, and one in every sequence holds exactly 1024.
All inputs are finite; a program needn't handle non-finite values.
Results may differ from a plain program's by a relative error of at most 0.017.
Values may be sent and summed in bfloat16 or wider, within the bound.
No kernel may reach another device: no remote copies, remote signals or barrier semaphores. Data moves between devices by JAX's collectives and lax.ppermute only.
A program may use at most 192 MiB of HBM per device.

v0:
```python
import math
import jax
import jax.numpy as jnp
from jax import lax
from jax.sharding import PartitionSpec as P

HEADS = 12
HEAD_DIM = 64
DOC_MOST = 1024
NEG_BIG = -1e30
EPSILON = 1e-05


def passed_along(block, axis, distance):
    devices = range(lax.axis_size(axis))
    route = [(i - distance, i) for i in devices if i - distance in devices]
    return lax.ppermute(block, axis, route)


def smooth_gate(values):
    return jax.nn.gelu(values, approximate=True)


def norm_rows(values):
    center = values - jnp.mean(values, axis=-1, keepdims=True)
    scale = lax.rsqrt(jnp.mean(center * center, axis=-1, keepdims=True) + EPSILON)
    return (center * scale, scale)


def norm_back(grad_normed, normed, scale):
    inner = jnp.mean(grad_normed * normed, axis=-1, keepdims=True)
    return scale * (grad_normed - jnp.mean(grad_normed, axis=-1, keepdims=True) - normed * inner)


def over_blocks(step, state, pieces, first):
    length = pieces[0].shape[0]
    stride = math.gcd(length, 512)

    def advance(index, current):
        begin = index * stride
        parts = tuple((piece for piece in pieces))
        return step(current, parts, first + begin)

    return lax.fori_loop(0, length // stride, advance, state)


def allowed_pairs(query_pos, query_seg, key_pos, key_seg, limit):
    inside = (key_pos[None, :] >= 0) & (query_pos[:, None] < limit)
    return (
        inside & (key_pos[None, :] <= query_pos[:, None]) & (key_seg[None, :] == query_seg[:, None])
    )


def head_split(rows):
    return rows.reshape(rows.shape[0], HEADS, HEAD_DIM)


def forward_step(queries, query_pos, query_seg, segment_row, limit):
    width = HEADS * HEAD_DIM
    scale = HEAD_DIM ** (-0.5)

    def step(state, parts, first):
        run_max, run_total, weighted = state
        count = parts[0].shape[0]
        key_rows = head_split(parts[0][:, :width])
        value_rows = head_split(parts[0][:, width:])
        key_pos = first + jnp.arange(count, dtype=jnp.int32)
        key_seg = lax.dynamic_slice_in_dim(segment_row, first, count, 0)
        allowed = allowed_pairs(query_pos, query_seg, key_pos, key_seg, limit)[None]
        scores = (
            jnp.einsum("qhd,khd->hqk", queries, key_rows, preferred_element_type=jnp.float32)
            * scale
        )
        new_max = jnp.maximum(run_max, jnp.max(jnp.where(allowed, scores, NEG_BIG), axis=-1))
        shares = jnp.where(allowed, jnp.exp(scores - new_max[..., None]), 0.0)
        factor = jnp.exp(run_max - new_max)
        run_total = run_total * factor + jnp.sum(shares, axis=-1)
        update = jnp.einsum(
            "hqk,khd->qhd",
            shares.astype(jnp.bfloat16),
            value_rows,
            preferred_element_type=jnp.float32,
        )
        weighted = weighted * factor.T[:, :, None] + update
        return (new_max, run_total, weighted)

    return step


def backward_core(queries, grad_heads, log_total, delta, key_rows, value_rows, allowed):
    scale = HEAD_DIM ** (-0.5)
    scores = (
        jnp.einsum("qhd,khd->hqk", queries, key_rows, preferred_element_type=jnp.float32) * scale
    )
    soft = jnp.where(allowed[None], jnp.exp(scores - log_total[..., None]), 0.0)
    grad_soft = jnp.einsum(
        "qhd,khd->hqk", grad_heads, value_rows, preferred_element_type=jnp.float32
    )
    grad_scores = (soft * (grad_soft - delta[..., None])).astype(jnp.bfloat16)
    return (soft.astype(jnp.bfloat16), grad_scores)


def query_step(queries, grad_heads, log_total, delta, query_pos, query_seg, segment_row, limit):
    width = HEADS * HEAD_DIM
    scale = HEAD_DIM ** (-0.5)

    def step(state, parts, first):
        count = parts[0].shape[0]
        key_rows = head_split(parts[0][:, :width])
        value_rows = head_split(parts[0][:, width:])
        key_pos = first + jnp.arange(count, dtype=jnp.int32)
        key_seg = lax.dynamic_slice_in_dim(segment_row, first, count, 0)
        allowed = allowed_pairs(query_pos, query_seg, key_pos, key_seg, limit)
        soft_low, grad_scores = backward_core(
            queries, grad_heads, log_total, delta, key_rows, value_rows, allowed
        )
        grad_query = (
            jnp.einsum("hqk,khd->qhd", grad_scores, key_rows, preferred_element_type=jnp.float32)
            * scale
        )
        grad_q, grad_block = state
        grad_keys = (
            jnp.einsum("hqk,qhd->khd", grad_scores, queries, preferred_element_type=jnp.float32)
            * scale
        )
        grad_values = jnp.einsum(
            "hqk,qhd->khd", soft_low, grad_heads, preferred_element_type=jnp.float32
        )
        joined = jnp.concatenate(
            [grad_keys.reshape(count, width), grad_values.reshape(count, width)], axis=1
        )
        current = grad_block
        grad_block = current + joined
        return (grad_q + grad_query, grad_block)

    return step


def on_device(
    layer_input,
    token_ids,
    segment_ids,
    hash_table,
    first_gain,
    first_bias,
    second_gain,
    second_bias,
    w_qkv,
    w_out,
    w_up,
    w_down,
    cotangent,
):
    local_len = layer_input.shape[1]
    width = layer_input.shape[2]
    sources = lax.axis_size("exp")
    local_exp = w_up.shape[0]
    experts_total = local_exp * sources
    capacity = 2 * local_len // experts_total
    total_len = local_len * lax.axis_size("seq")
    reach_blocks = (DOC_MOST + local_len - 2) // local_len
    offset = lax.axis_index("seq") * local_len
    segment_row = segment_ids[0]
    query_pos = offset + jnp.arange(local_len, dtype=jnp.int32)
    query_seg = lax.dynamic_slice_in_dim(segment_row, offset, local_len, 0)
    inputs = layer_input[0].astype(jnp.float32)
    normed_one, scale_one = norm_rows(inputs)
    attn_in = (normed_one * first_gain + first_bias).astype(jnp.bfloat16)
    projected = jnp.dot(attn_in, w_qkv, preferred_element_type=jnp.float32).astype(jnp.bfloat16)
    queries = head_split(projected[:, :width])
    key_value = projected[:, width:]
    kv_blocks = [key_value]
    moving = key_value
    for hop_index in range(reach_blocks):
        moving = passed_along(moving, "seq", 1)
        kv_blocks.append(moving)
    state = (
        jnp.full((HEADS, local_len), NEG_BIG, jnp.float32),
        jnp.zeros((HEADS, local_len), jnp.float32),
        jnp.zeros((local_len, HEADS, HEAD_DIM), jnp.float32),
    )
    attend = forward_step(queries, query_pos, query_seg, segment_row, total_len)
    for block_index in range(reach_blocks + 1):
        state = over_blocks(
            attend, state, (kv_blocks[block_index],), offset - block_index * local_len
        )
    run_max, run_total, weighted = state
    attn_exact = (weighted / run_total.T[:, :, None]).reshape(local_len, width)
    log_total = run_max + jnp.log(run_total)
    attn_rows = attn_exact.astype(jnp.bfloat16)
    resid = inputs + jnp.dot(attn_rows, w_out, preferred_element_type=jnp.float32)
    normed_two, scale_two = norm_rows(resid)
    ffn_in = (normed_two * second_gain + second_bias).astype(jnp.bfloat16)
    choice_ids = hash_table[token_ids[0]]
    order = jnp.argsort(choice_ids, stable=True)
    places = jnp.argsort(order, stable=True)
    expert_grid = jnp.arange(experts_total, dtype=jnp.int32)
    matches = choice_ids[:, None] == expert_grid[None, :]
    counts = jnp.sum(matches.astype(jnp.int32), axis=0)
    starts = jnp.cumsum(counts) - counts
    slot_grid = jnp.arange(capacity, dtype=jnp.int32)
    gather_index = order[jnp.minimum(starts[:, None] + slot_grid[None, :], local_len - 1)]
    filled = (slot_grid[None, :] < counts[:, None])[:, :, None]
    own_start = jnp.sum(jnp.where(matches, starts[None, :], 0), axis=1)
    token_slot = choice_ids * capacity + places - own_start
    send = jnp.where(filled, ffn_in[gather_index], jnp.zeros((), jnp.bfloat16))
    received = lax.all_to_all(send, "exp", split_axis=0, concat_axis=0, tiled=True)
    grouped = received.reshape(sources, local_exp, capacity, width)
    pre_act = jnp.einsum("secd,edf->secf", grouped, w_up, preferred_element_type=jnp.float32)
    activated, gate_pullback = jax.vjp(smooth_gate, pre_act)
    hidden = activated.astype(jnp.bfloat16)
    expert_out = jnp.einsum(
        "secf,efd->secd", hidden, w_down, preferred_element_type=jnp.float32
    ).astype(jnp.bfloat16)
    returned = lax.all_to_all(
        expert_out.reshape(experts_total, capacity, width),
        "exp",
        split_axis=0,
        concat_axis=0,
        tiled=True,
    )
    ffn_rows = returned.reshape(experts_total * capacity, width)[token_slot].astype(jnp.float32)
    layer_output = (resid + ffn_rows).astype(jnp.bfloat16)
    grad_final = cotangent[0].astype(jnp.float32)
    grad_branch = grad_final.astype(jnp.bfloat16)
    grad_send = jnp.where(filled, grad_branch[gather_index], jnp.zeros((), jnp.bfloat16))
    grad_received = lax.all_to_all(
        grad_send, "exp", split_axis=0, concat_axis=0, tiled=True
    ).reshape(sources, local_exp, capacity, width)
    grad_w_down = jnp.einsum(
        "secf,secd->efd", hidden, grad_received, preferred_element_type=jnp.float32
    )
    grad_hidden = jnp.einsum(
        "secd,efd->secf", grad_received, w_down, preferred_element_type=jnp.float32
    )
    grad_pre = gate_pullback(grad_hidden)[0].astype(jnp.bfloat16)
    grad_w_up = jnp.einsum("secd,secf->edf", grouped, grad_pre, preferred_element_type=jnp.float32)
    grad_slots = jnp.einsum(
        "secf,edf->secd", grad_pre, w_up, preferred_element_type=jnp.float32
    ).astype(jnp.bfloat16)
    grad_back = lax.all_to_all(
        grad_slots.reshape(experts_total, capacity, width),
        "exp",
        split_axis=0,
        concat_axis=0,
        tiled=True,
    )
    grad_ffn_in = grad_back.reshape(experts_total * capacity, width)[token_slot].astype(jnp.float32)
    grad_second_gain = jnp.sum(grad_ffn_in * normed_two, axis=0)
    grad_second_bias = jnp.sum(grad_ffn_in, axis=0)
    grad_resid = grad_final + norm_back(grad_ffn_in * second_gain, normed_two, scale_two)
    grad_attn = grad_resid.astype(jnp.bfloat16)
    grad_w_out = jnp.einsum("cd,ce->de", attn_rows, grad_attn, preferred_element_type=jnp.float32)
    grad_out_rows = jnp.einsum(
        "ce,de->cd", grad_attn, w_out, preferred_element_type=jnp.float32
    ).astype(jnp.bfloat16)
    grad_heads = head_split(grad_out_rows)
    delta = jnp.sum(grad_heads.astype(jnp.float32) * head_split(attn_exact), axis=-1).T
    back_blocks = [key_value]
    moving = key_value
    for hop_index in range(reach_blocks):
        moving = passed_along(moving, "seq", 1)
        back_blocks.append(moving)
    grad_query = jnp.zeros((local_len, HEADS, HEAD_DIM), jnp.float32)
    block_grads = []
    for block_index in range(reach_blocks + 1):
        base = offset - block_index * local_len
        back_step = query_step(
            queries, grad_heads, log_total, delta, query_pos, query_seg, segment_row, total_len
        )
        grad_query, grad_block = over_blocks(
            back_step,
            (grad_query, jnp.zeros((local_len, 2 * width), jnp.float32)),
            (back_blocks[block_index],),
            base,
        )
        block_grads.append(grad_block)
    carried = block_grads[reach_blocks]
    for block_index in range(reach_blocks, 0, -1):
        carried = (
            passed_along(carried.astype(jnp.bfloat16), "seq", -1).astype(carried.dtype)
            + block_grads[block_index - 1]
        )
    grad_proj = jnp.concatenate([grad_query.reshape(local_len, width), carried], axis=1).astype(
        jnp.bfloat16
    )
    grad_w_qkv = jnp.einsum("cd,ce->de", attn_in, grad_proj, preferred_element_type=jnp.float32)
    grad_attn_in = jnp.einsum("ce,de->cd", grad_proj, w_qkv, preferred_element_type=jnp.float32)
    grad_first_gain = jnp.sum(grad_attn_in * normed_one, axis=0)
    grad_first_bias = jnp.sum(grad_attn_in, axis=0)
    grad_input = grad_resid + norm_back(grad_attn_in * first_gain, normed_one, scale_one)
    dense = lax.psum(
        (
            grad_w_qkv,
            grad_w_out,
            grad_first_gain,
            grad_first_bias,
            grad_second_gain,
            grad_second_bias,
        ),
        ("seq", "exp"),
    )
    expert_sums = (
        lax.psum(grad_w_up.astype(jnp.bfloat16), "seq").astype(jnp.float32),
        lax.psum(grad_w_down.astype(jnp.bfloat16), "seq").astype(jnp.float32),
    )
    return (
        layer_output[None],
        grad_input[None],
        dense[0],
        dense[1],
        dense[2],
        dense[3],
        dense[4],
        dense[5],
        expert_sums[0],
        expert_sums[1],
    )


def solution(mesh):
    in_specs = (
        P("exp", "seq", None),
        P("exp", "seq"),
        P("exp", None),
        P(),
        P(),
        P(),
        P(),
        P(),
        P(),
        P(),
        P("exp", None, None),
        P("exp", None, None),
        P("exp", "seq", None),
    )
    out_specs = (
        P("exp", "seq", None),
        P("exp", "seq", None),
        P(),
        P(),
        P(),
        P(),
        P(),
        P(),
        P("exp", None, None),
        P("exp", None, None),
    )
    return jax.shard_map(
        on_device, mesh=mesh, in_specs=in_specs, out_specs=out_specs, check_vma=False
    )
```

profile of v0, /device:TPU:0, one launch (start us, length us, event | category | flops | bytes accessed | tf_op | source)
XLA Modules:
  0.0 691.7 jit_solution(2766946564341442537)
XLA Ops:
  10.2 3.3 convolution_convert_fusion
  16.2 3.6 collective-permute-start
  19.8 3.4 gather_fusion
  23.9 3.8 sort.31
  27.7 11.3 %gather_fusion.1 = s32[1024]{0:T(1024)} fusion(s32[512]{0:T(512)S(1)} %get-tuple-element.163, s32[1024]{0:T(1024)S(1)} %broadcast_clamp_fusion.1), kind=kCustom, calls=%fused_computation.1 | custom fusion | bytes 12288 | tf_op jit(solution)/shard_map/gather | solution.py:202
  40.5 3.1 fusion.155
  45.9 4.5 collective-permute-start.1
  56.3 2.3 copy.84
  58.6 7.0 %gather_fusion.4 = bf16[1024,768]{1,0:T(8,128)(2,1)} fusion(bf16[512,768]{1,0:T(8,128)(2,1)} %bitcast.289, s32[1024]{0:T(1024)S(1)} %broadcast_clamp_fusion), kind=kCustom, calls=%fused_computation.4 | custom fusion | bytes 3149824 | tf_op jit(solution)/shard_map/gather | solution.py:226
  65.6 8.6 %select_reduce_fusion.2 = (f32[12,512]{1,0:T(8,128)}, f32[12,512,512]{1,2,0:T(8,128)}) fusion(pred[512,512]{0,1:T(8,128)(4,1)} %get-tuple-element.239, bf16[512,12,64]{0,2,1:T(8,128)(2,1)} %bitcast.294, bf16[512,12,64]{0,2,1:T(8,128)(2,1)} %bitcast.302), kind=kOutput, calls=%fused_computation.33 | convolution fusion | flops 412084224 | bytes 14442496 | tf_op jit(solution)/shard_map/while/body/eval_jaxpr/qhd,khd->hqk/dot_general | solution.py:71
  74.2 2.6 fusion.157
  79.1 2.3 copy.89
  81.5 8.6 %select_reduce_fusion.1 = (f32[12,512]{1,0:T(8,128)}, f32[12,512,512]{1,2,0:T(8,128)}) fusion(pred[512,512]{0,1:T(8,128)(4,1)} %get-tuple-element.241, bf16[512,12,64]{0,2,1:T(8,128)(2,1)} %bitcast.295, bf16[512,12,64]{0,2,1:T(8,128)(2,1)} %bitcast.300), kind=kOutput, calls=%fused_computation.31 | convolution fusion | flops 412084224 | bytes 14442496 | tf_op jit(solution)/shard_map/while/body/eval_jaxpr/qhd,khd->hqk/dot_general | solution.py:71
  90.1 2.6 fusion.156
  97.3 8.1 %select_reduce_fusion = (f32[12,512]{1,0:T(8,128)S(1)}, f32[12,512,512]{1,2,0:T(8,128)}) fusion(pred[512,512]{0,1:T(8,128)(4,1)} %get-tuple-element.240, bf16[512,12,64]{0,2,1:T(8,128)(2,1)} %bitcast.296, bf16[512,12,64]{0,2,1:T(8,128)(2,1)} %bitcast.304), kind=kOutput, calls=%fused_computation.29 | convolution fusion | flops 412084224 | bytes 14442496 | tf_op jit(solution)/shard_map/while/body/eval_jaxpr/qhd,khd->hqk/dot_general | solution.py:71
  106.1 7.3 %fusion.13 = f32[12,512]{1,0:T(8,128)S(1)} fusion(f32[12,512,512]{1,2,0:T(8,128)} %get-tuple-element.247, f32[12,512]{1,0:T(8,128)S(1)} %get-tuple-element.210, pred[512,512]{0,1:T(8,128)(4,1)S(1)} %copy-done.19), kind=kLoop, calls=%fused_computation.36 | loop fusion | flops 12576768 | bytes 12894208 | tf_op jit(solution)/shard_map/while/body/eval_jaxpr/reduce_sum | solution.py:77
  113.4 20.8 %fusion.36 = f32[12,64,512]{2,1,0:T(8,128)} fusion(bf16[512,12,64]{0,2,1:T(8,128)(2,1)} %bitcast.324, f32[12,512,512]{1,2,0:T(8,128)} %get-tuple-element.247, f32[12,512]{1,0:T(8,128)S(1)} %get-tuple-element.210, pred[512,512]{0,1:T(8,128)(4,1)} %get-tuple-element.241), kind=kOutput, calls=%fused_computation.57 | convolution fusion | flops 415236096 | bytes 15228928 | tf_op jit(solution)/shard_map/while/body/eval_jaxpr/hqk,khd->qhd/dot_general | solution.py:78
  134.2 3.5 fusion.11
  137.8 4.7 fusion.38
  142.5 7.3 %fusion.15 = f32[12,512]{1,0:T(8,128)S(1)} fusion(f32[12,512,512]{1,2,0:T(8,128)} %get-tuple-element.245, f32[12,512]{1,0:T(8,128)} %get-tuple-element.196, pred[512,512]{0,1:T(8,128)(4,1)} %get-tuple-element.240), kind=kLoop, calls=%fused_computation.38 | loop fusion | flops 12576768 | bytes 12894208 | tf_op jit(solution)/shard_map/while/body/eval_jaxpr/reduce_sum | solution.py:77
  150.0 8.8 %fusion.158 = (bf16[512,12,64]{0,2,1:T(8,128)(2,1)S(1)}, f32[512,12,64]{0,2,1:T(8,128)}) fusion(f32[512,12]{0,1:T(8,128)S(1)} %get-tuple-element.194, bf16[512,12,64]{0,2,1:T(8,128)(2,1)S(1)} %bitcast.326, f32[12,512,512]{1,2,0:T(8,128)} %get-tuple-element.245, f32[12,512]{1,0:T(8,128)S(1)} %copy-done.37, pred[512,512]{0,1:T(8,128)(4,1)S(1)} %copy-done.21, ...), kind=kOutput, calls=%fused_computation.216 | convolution fusion | flops 417988608 | bytes 19259392 | tf_op jit(solution)/shard_map/while/body/eval_jaxpr/hqk,khd->qhd/dot_general | solution.py:78
  162.6 7.0 %gather_fusion.2 = bf16[1024,768]{1,0:T(8,128)(2,1)} fusion(bf16[512,768]{1,0:T(8,128)(2,1)} %add_convert_fusion.1, s32[1024]{0:T(1024)} %copy-done.44), kind=kCustom, calls=%fused_computation.2 | custom fusion | bytes 3149824 | tf_op jit(solution)/shard_map/gather | solution.py:206
  169.7 3.8 broadcast_select_fusion
  173.5 4.9 all-to-all-start
  179.0 4.4 sort.32
  186.3 28.2 %all-to-all-done = bf16[4,256,768]{2,1,0:T(8,128)(2,1)} async-done(((bf16[4,256,768]{2,1,0:T(8,128)(2,1)}), bf16[4,256,768]{2,1,0:T(8,128)(2,1)}, u32[]{:S(2)}, u32[]{:S(2)}) %all-to-all-start) | async-done | bytes 1572896 | tf_op jit(solution)/shard_map/all_to_all | solution.py:207
  214.5 4.4 all-to-all-start.2
  218.9 7.4 %fusion.54 = f32[4,256,3072]{2,1,0:T(8,128)S(1)} fusion(bf16[4,256,768]{2,1,0:T(8,128)(2,1)} %all-to-all-done, bf16[1,768,3072]{2,1,0:T(8,128)(2,1)} %param.23), kind=kOutput, calls=%fused_computation.69 | convolution fusion | flops 4831838208 | bytes 18874368 | tf_op jit(solution)/shard_map/secd,edf->secf/dot_general | solution.py:209
  226.3 4.5 copy-done.64
  230.7 10.8 %fusion.77 = bf16[4,256,768]{2,1,0:T(8,128)(2,1)} fusion(bf16[1,3072,768]{2,1,0:T(8,128)(2,1)} %param.24, f32[4,256,3072]{2,1,0:T(8,128)S(1)} %fusion.54), kind=kOutput, calls=%fused_computation.95 | convolution fusion | flops 4860936192 | bytes 18874368 | tf_op jit(solution)/shard_map/secf,efd->secd/dot_general | solution.py:212
  241.5 13.9 %all-to-all-done.2 = bf16[4,256,768]{2,1,0:T(8,128)(2,1)} async-done(((bf16[4,256,768]{2,1,0:T(8,128)(2,1)}), bf16[4,256,768]{2,1,0:T(8,128)(2,1)}, u32[]{:S(2)}, u32[]{:S(2)}) %all-to-all-start.2) | async-done | bytes 1572896 | tf_op jit(solution)/shard_map/all_to_all | solution.py:227
  255.4 4.8 all-to-all-start.1
  260.2 15.3 %fusion.6 = bf16[4,1,256,3072]{3,2,0,1:T(8,128)(2,1)S(1)} fusion(f32[4,256,3072]{2,1,0:T(8,128)} %copy-done.64, bf16[4,256,768]{2,1,0:T(8,128)(2,1)} %all-to-all-done.2, bf16[1,3072,768]{2,1,0:T(8,128)(2,1)} %param.24), kind=kOutput, calls=%fused_computation.14 | convolution fusion | flops 4894752768 | bytes 25165824 | tf_op jit(solution)/shard_map/secd,efd->secf/dot_general | solution.py:233
  275.5 8.5 %fusion.82 = bf16[4,256,768]{2,1,0:T(8,128)(2,1)} fusion(bf16[1,768,3072]{2,1,0:T(8,128)(2,1)} %param.23, bf16[4,1,256,3072]{3,2,0,1:T(8,128)(2,1)S(1)} %fusion.6), kind=kOutput, calls=%fused_computation.96 | convolution fusion | flops 4832624640 | bytes 12582912 | tf_op jit(solution)/shard_map/secf,edf->secd/dot_general | solution.py:238
  284.1 8.2 %fusion.56 = bf16[1,768,3072]{2,1,0:T(8,128)(2,1)} fusion(bf16[4,256,768]{2,1,0:T(8,128)(2,1)} %all-to-all-done, bf16[4,1,256,3072]{3,2,0,1:T(8,128)(2,1)S(1)} %fusion.6), kind=kOutput, calls=%fused_computation.71 | convolution fusion | flops 4834197504 | bytes 12582912 | tf_op jit(solution)/shard_map/secd,secf->edf/dot_general | solution.py:237
  292.3 4.4 all-to-all-done.1
  296.7 4.4 all-to-all-start.3
  301.1 12.0 %fusion.59 = bf16[1,3072,768]{2,1,0:T(8,128)(2,1)} fusion(bf16[4,256,768]{2,1,0:T(8,128)(2,1)} %all-to-all-done.2, f32[4,256,3072]{2,1,0:T(8,128)} %copy-done.64), kind=kOutput, calls=%fused_computation.72 | convolution fusion | flops 4862509056 | bytes 18874368 | tf_op jit(solution)/shard_map/secf,secd->efd/dot_general | solution.py:230
  313.4 4.7 gather_fusion.3
  318.1 19.5 %all-to-all-done.3 = bf16[4,256,768]{2,1,0:T(8,128)(2,1)} async-done(((bf16[4,256,768]{2,1,0:T(8,128)(2,1)}), bf16[4,256,768]{2,1,0:T(8,128)(2,1)}, u32[]{:S(2)}, u32[]{:S(2)}) %all-to-all-start.3) | async-done | bytes 1572896 | tf_op jit(solution)/shard_map/all_to_all | solution.py:241
  337.6 4.7 gather_fusion.5
  342.3 3.1 fusion.102
  345.4 3.7 fusion.100
  356.2 8.6 %fusion.110 = bf16[12,64,512]{2,1,0:T(8,128)(2,1)} fusion(bf16[512,12,64]{0,2,1:T(8,128)(2,1)} %bitcast.311, f32[12,512,512]{1,2,0:T(8,128)} %get-tuple-element.245, f32[12,512]{1,0:T(8,128)} %log_add_fusion, pred[512,512]{0,1:T(8,128)(4,1)} %get-tuple-element.240), kind=kOutput, calls=%fused_computation.132 | convolution fusion | flops 415629312 | bytes 14442496 | tf_op jit(solution)/shard_map/while/body/eval_jaxpr/hqk,qhd->khd/dot_general | solution.py:126
  364.8 7.8 %multiply_convert_fusion = bf16[12,512,512]{1,2,0:T(8,128)(2,1)S(1)} fusion(f32[12,512,512]{1,2,0:T(8,128)} %get-tuple-element.245, f32[12,512]{1,0:T(8,128)S(1)} %bitcast.331, f32[12,512]{1,0:T(8,128)S(1)} %copy-done.47, pred[512,512]{0,1:T(8,128)(4,1)S(1)} %copy-done.22, bf16[512,12,64]{0,2,1:T(8,128)(2,1)S(1)} %bitcast.312, ...), kind=kOutput, calls=%fused_computation.22 | convolution fusion | flops 421527552 | bytes 20758528 | tf_op jit(solution)/shard_map/while/body/eval_jaxpr/qhd,khd->hqk/dot_general | solution.py:96
  372.7 7.6 %multiply_convert_fusion.2 = bf16[12,512,512]{1,2,0:T(8,128)(2,1)S(1)} fusion(f32[12,512,512]{1,2,0:T(8,128)} %get-tuple-element.262, f32[12,512]{1,0:T(8,128)S(1)} %bitcast.332, f32[12,512]{1,0:T(8,128)S(1)} %copy-done.47, pred[512,512]{0,1:T(8,128)(4,1)} %get-tuple-element.239, bf16[512,12,64]{0,2,1:T(8,128)(2,1)S(1)} %bitcast.313, ...), kind=kOutput, calls=%fused_computation.26 | convolution fusion | flops 421527552 | bytes 20758528 | tf_op jit(solution)/shard_map/while/body/eval_jaxpr/qhd,khd->hqk/dot_general | solution.py:96
  380.3 2.4 fusion.160
  382.7 3.1 convolution_multiply_fusion
  385.8 8.0 %multiply_convert_fusion.1 = bf16[12,512,512]{1,2,0:T(8,128)(2,1)S(1)} fusion(f32[12,512,512]{1,2,0:T(8,128)} %get-tuple-element.247, f32[12,512]{1,0:T(8,128)S(1)} %bitcast.333, f32[12,512]{1,0:T(8,128)S(1)} %copy-done.47, pred[512,512]{0,1:T(8,128)(4,1)} %get-tuple-element.241, bf16[512,12,64]{0,2,1:T(8,128)(2,1)S(1)} %bitcast.314, ...), kind=kOutput, calls=%fused_computation.24 | convolution fusion | flops 421527552 | bytes 20758528 | tf_op jit(solution)/shard_map/while/body/eval_jaxpr/qhd,khd->hqk/dot_general | solution.py:96
  398.5 3.1 convolution_multiply_fusion.1
  401.7 2.3 fusion.161
  404.0 6.1 fusion.30
  410.2 3.4 fusion.64
  419.8 3.6 fusion.32
  423.5 14.7 %collective-permute-done.3 = bf16[512,1536]{0,1:T(8,128)(2,1)} collective-permute-done((bf16[512,1536]{0,1:T(8,128)(2,1)}, bf16[512,1536]{0,1:T(8,128)(2,1)}, u32[]{:S(2)}, u32[]{:S(2)}) %collective-permute-start.3) | collective-permute-done | bytes 1572896 | tf_op jit(solution)/shard_map/ppermute | solution.py:17
  441.4 5.3 fusion.106
  446.7 23.3 %all-reduce.8.cloned.1.call-done = (bf16[1,768,3072]{2,1,0:T(8,128)(2,1)}, bf16[1,3072,768]{2,1,0:T(8,128)(2,1)}) async-done(((bf16[1,768,3072]{2,1,0:T(8,128)(2,1)}, bf16[1,3072,768]{2,1,0:T(8,128)(2,1)}), (bf16[1,768,3072]{2,1,0:T(8,128)(2,1)}, bf16[1,3072,768]{2,1,0:T(8,128)(2,1)})) %all-reduce.8.cloned.1.call-update) | async-done | bytes 9437200 | tf_op jit(solution)/shard_map/psum | solution.py:304
  470.0 7.5 %convert_element_type.162 = f32[1,768,3072]{2,1,0:T(8,128)} convert(bf16[1,768,3072]{2,1,0:T(8,128)(2,1)} %get-tuple-element.192) | non-fusion elementwise | flops 2359296 | bytes 14155776 | tf_op jit(solution)/shard_map/convert_element_type | solution.py:304
  477.6 4.5 convert_element_type.165
  482.1 4.2 fusion.96
  486.2 55.8 %all-reduce = (f32[768]{0:T(1024)}, f32[768]{0:T(1024)}, f32[768]{0:T(1024)}, f32[768]{0:T(1024)}) all-reduce(f32[768]{0:T(1024)} %get-tuple-element.167, f32[768]{0:T(1024)} %get-tuple-element.170, f32[768]{0:T(1024)S(1)} %get-tuple-element.165, f32[768]{0:T(1024)S(1)} %copy-done.50), channel_id=1, replica_groups=mesh['seq'=8,'exp'=4] {'seq','exp'}, use_global_device_ids=true, to_apply=%region_23.24 | all-reduce | flops 3072 | bytes 24576 | tf_op jit(solution)/shard_map/psum | solution.py:292
  543.4 4.0 fusion.95
  547.3 129.1 %all-reduce.6.cloned.1.call-done = (f32[768,2304]{1,0:T(8,128)}, f32[768,768]{1,0:T(8,128)}) async-done(((f32[768,2304]{1,0:T(8,128)}, f32[768,768]{1,0:T(8,128)}), (f32[768,2304]{1,0:T(8,128)}, f32[768,768]{1,0:T(8,128)})) %all-reduce.6.cloned.1.call-update) | async-done | bytes 9437200 | tf_op jit(solution)/shard_map/psum | solution.py:292
  676.4 6.6 copy.132
  (207 shorter events, 55.1 us)
Async XLA Ops:
  8.7 4.9 copy-start.48
  10.2 9.6 %copy-start.57 = (s32[1,512]{1,0:T(1,128)S(1)}, s32[1,512]{1,0:T(1,128)}, u32[]{:S(2)}) copy-start(s32[1,512]{1,0:T(1,128)} %param.14) | copy-start | bytes 6148
  16.2 29.7 %collective-permute-start = (bf16[512,1536]{1,0:T(8,128)(2,1)}, bf16[512,1536]{1,0:T(8,128)(2,1)}, u32[]{:S(2)}, u32[]{:S(2)}) collective-permute-start(bf16[512,1536]{1,0:T(8,128)(2,1)} %slice.67), channel_id=1, source_target_pairs={{0,4},{4,8},{8,12},{12,16},{16,20},{20,24},{24,28},{1,5},{5,9},{9,... | collective-permute-start | bytes 4718600 | tf_op jit(solution)/shard_map/ppermute | solution.py:17
  40.5 18.1 %copy-start.44 = (s32[1024]{0:T(1024)}, s32[1024]{0:T(1024)S(1)}, u32[]{:S(2)}) copy-start(s32[1024]{0:T(1024)S(1)} %broadcast_clamp_fusion) | copy-start | bytes 12292
  45.9 44.2 %collective-permute-start.1 = (bf16[512,1536]{1,0:T(8,128)(2,1)}, bf16[512,1536]{1,0:T(8,128)(2,1)}, u32[]{:S(2)}, u32[]{:S(2)}) collective-permute-start(bf16[512,1536]{1,0:T(8,128)(2,1)} %collective-permute-done), channel_id=1, source_target_pairs={{0,4},{4,8},{8,12},{12,16},{16,20},{20,24},{24,28},{1,5},{5,9},{9,... | collective-permute-start | bytes 4718600 | tf_op jit(solution)/shard_map/ppermute | solution.py:17
  97.3 8.1 %copy-start.33 = (f32[12,512]{1,0:T(8,128)S(1)}, f32[12,512]{1,0:T(8,128)}, u32[]{:S(2)}) copy-start(f32[12,512]{1,0:T(8,128)} %get-tuple-element.248) | copy-start | bytes 73732
  97.3 8.1 %copy-start.39 = (f32[12,512]{1,0:T(8,128)S(1)}, f32[12,512]{1,0:T(8,128)}, u32[]{:S(2)}) copy-start(f32[12,512]{1,0:T(8,128)} %get-tuple-element.246) | copy-start | bytes 73732
  97.3 8.8 %copy-start.19 = (pred[512,512]{0,1:T(8,128)(4,1)S(1)}, pred[512,512]{0,1:T(8,128)(4,1)}, u32[]{:S(2)}) copy-start(pred[512,512]{0,1:T(8,128)(4,1)} %get-tuple-element.241) | copy-start | bytes 786436
  105.4 7.9 %copy-start.41 = (f32[12,512]{1,0:T(8,128)}, f32[12,512]{1,0:T(8,128)S(1)}, u32[]{:S(2)}) copy-start(f32[12,512]{1,0:T(8,128)S(1)} %get-tuple-element.244) | copy-start | bytes 73732
  106.1 7.3 %copy-start.38 = (f32[12,512]{1,0:T(8,128)}, f32[12,512]{1,0:T(8,128)S(1)}, u32[]{:S(2)}) copy-start(f32[12,512]{1,0:T(8,128)S(1)} %get-tuple-element.210) | copy-start | bytes 73732
  106.1 28.1 %slice-start = ((s8[12582912]{0:T(1024)(128)(4,1)}), s8[4194304]{0:T(1024)(128)(4,1)S(1)}, s32[]{:S(2)}) async-start(s8[12582912]{0:T(1024)(128)(4,1)} %bitcast.290), calls=%async_computation.6 | async-start | bytes 8388608
  106.1 28.1 %slice-start.1 = ((s8[12582912]{0:T(1024)(128)(4,1)}), s8[4194304]{0:T(1024)(128)(4,1)S(1)}, s32[]{:S(2)}) async-start(s8[12582912]{0:T(1024)(128)(4,1)} %bitcast.290), calls=%async_computation.7 | async-start | bytes 8388608
  113.4 36.4 %copy-start.34 = (f32[12,512]{1,0:T(8,128)}, f32[12,512]{1,0:T(8,128)S(1)}, u32[]{:S(2)}) copy-start(f32[12,512]{1,0:T(8,128)S(1)} %fusion.13) | copy-start | bytes 73732
  113.4 20.8 %slice-start.2 = ((s8[12582912]{0:T(1024)(128)(4,1)}), s8[4194304]{0:T(1024)(128)(4,1)S(1)}, s32[]{:S(2)}) async-start(s8[12582912]{0:T(1024)(128)(4,1)} %bitcast.290), calls=%async_computation.8 | async-start | bytes 8388608
  137.8 12.1 %copy-start.35 = (f32[12,512]{1,0:T(8,128)}, f32[12,512]{1,0:T(8,128)S(1)}, u32[]{:S(2)}) copy-start(f32[12,512]{1,0:T(8,128)S(1)} %fusion.11) | copy-start | bytes 73732
  142.5 7.4 %copy-start.40 = (f32[12,512]{1,0:T(8,128)S(1)}, f32[12,512]{1,0:T(8,128)}, u32[]{:S(2)}) copy-start(f32[12,512]{1,0:T(8,128)} %get-tuple-element.246) | copy-start | bytes 73732
  142.5 7.4 %copy-start.42 = (f32[12,512]{1,0:T(8,128)S(1)}, f32[12,512]{1,0:T(8,128)}, u32[]{:S(2)}) copy-start(f32[12,512]{1,0:T(8,128)} %copy-done.41) | copy-start | bytes 73732
  142.5 7.4 %copy-start.21 = (pred[512,512]{0,1:T(8,128)(4,1)S(1)}, pred[512,512]{0,1:T(8,128)(4,1)}, u32[]{:S(2)}) copy-start(pred[512,512]{0,1:T(8,128)(4,1)} %get-tuple-element.240) | copy-start | bytes 786436
  142.5 7.4 %copy-start.28 = (bf16[512,768]{0,1:T(8,128)(2,1)S(1)}, bf16[512,768]{0,1:T(8,128)(2,1)}, u32[]{:S(2)}) copy-start(bf16[512,768]{0,1:T(8,128)(2,1)} %copy.92) | copy-start | bytes 2359300
  142.5 7.4 %copy-start.37 = (f32[12,512]{1,0:T(8,128)S(1)}, f32[12,512]{1,0:T(8,128)}, u32[]{:S(2)}) copy-start(f32[12,512]{1,0:T(8,128)} %get-tuple-element.196) | copy-start | bytes 73732
  142.5 7.4 %copy-start.62 = (f32[12,64,512]{2,1,0:T(8,128)S(1)}, f32[12,64,512]{2,1,0:T(8,128)}, u32[]{:S(2)}) copy-start(f32[12,64,512]{2,1,0:T(8,128)} %fusion.36) | copy-start | bytes 4718596
  142.5 7.4 %copy-start.63 = (f32[12,64,512]{2,1,0:T(8,128)S(1)}, f32[12,64,512]{2,1,0:T(8,128)}, u32[]{:S(2)}) copy-start(f32[12,64,512]{2,1,0:T(8,128)} %fusion.38) | copy-start | bytes 4718596
  149.9 8.9 %copy-start.36 = (f32[12,512]{1,0:T(8,128)}, f32[12,512]{1,0:T(8,128)S(1)}, u32[]{:S(2)}) copy-start(f32[12,512]{1,0:T(8,128)S(1)} %fusion.15) | copy-start | bytes 73732
  150.0 8.8 %copy-start.10 = (bf16[1,512,768]{2,1,0:T(8,128)(2,1)S(1)}, bf16[1,512,768]{2,1,0:T(8,128)(2,1)}, u32[]{:S(2)}) copy-start(bf16[1,512,768]{2,1,0:T(8,128)(2,1)} %param.13) | copy-start | bytes 2359300
  150.0 8.8 %copy-start.59 = (bf16[768,768]{1,0:T(8,128)(2,1)S(1)}, bf16[768,768]{1,0:T(8,128)(2,1)}, u32[]{:S(2)}) copy-start(bf16[768,768]{1,0:T(8,128)(2,1)} %param.22) | copy-start | bytes 3538948
  173.5 41.0 %all-to-all-start = ((bf16[4,256,768]{2,1,0:T(8,128)(2,1)}), bf16[4,256,768]{2,1,0:T(8,128)(2,1)}, u32[]{:S(2)}, u32[]{:S(2)}) async-start(bf16[4,256,768]{2,1,0:T(8,128)(2,1)} %get-tuple-element.243), calls=%async_computation | async-start | bytes 3145728 | tf_op jit(solution)/shard_map/all_to_all | solution.py:207
  214.5 40.9 %all-to-all-start.2 = ((bf16[4,256,768]{2,1,0:T(8,128)(2,1)}), bf16[4,256,768]{2,1,0:T(8,128)(2,1)}, u32[]{:S(2)}, u32[]{:S(2)}) async-start(bf16[4,256,768]{2,1,0:T(8,128)(2,1)} %get-tuple-element.242), calls=%async_computation.2 | async-start | bytes 3145728 | tf_op jit(solution)/shard_map/all_to_all | solution.py:227
  226.3 4.5 copy-start.64
  255.4 41.3 %all-to-all-start.1 = ((bf16[4,256,768]{2,1,0:T(8,128)(2,1)}), bf16[4,256,768]{2,1,0:T(8,128)(2,1)}, u32[]{:S(2)}, u32[]{:S(2)}) async-start(bf16[4,256,768]{2,1,0:T(8,128)(2,1)} %fusion.77), calls=%async_computation.1 | async-start | bytes 3145728 | tf_op jit(solution)/shard_map/all_to_all | solution.py:215
  296.7 40.9 %all-to-all-start.3 = ((bf16[4,256,768]{2,1,0:T(8,128)(2,1)}), bf16[4,256,768]{2,1,0:T(8,128)(2,1)}, u32[]{:S(2)}, u32[]{:S(2)}) async-start(bf16[4,256,768]{2,1,0:T(8,128)(2,1)} %fusion.82), calls=%async_computation.3 | async-start | bytes 3145728 | tf_op jit(solution)/shard_map/all_to_all | solution.py:241
  301.1 169.0 %all-reduce.8.cloned.1.call-start = ((), (), s32[]{:S(2)}) async-start(), calls=%async_computation.5 | async-start | bytes 18874368 | tf_op jit(solution)/shard_map/psum | solution.py:304
  313.2 363.2 %all-reduce.6.cloned.1.call-start = ((), (), s32[]{:S(2)}) async-start(), calls=%async_computation.4 | async-start | bytes 18874368 | tf_op jit(solution)/shard_map/psum | solution.py:292
  318.1 24.2 %copy-start.46 = (f32[512]{0:T(512)S(1)}, f32[512]{0:T(512)}, u32[]{:S(2)}) copy-start(f32[512]{0:T(512)} %copy-done.45) | copy-start | bytes 6148
  342.3 8.0 %copy-start.60 = (bf16[768,768]{1,0:T(8,128)(2,1)S(1)}, bf16[768,768]{1,0:T(8,128)(2,1)}, u32[]{:S(2)}) copy-start(bf16[768,768]{1,0:T(8,128)(2,1)} %param.22) | copy-start | bytes 3538948
  356.2 8.6 %copy-start.17 = (bf16[512,768]{0,1:T(8,128)(2,1)S(1)}, bf16[512,768]{0,1:T(8,128)(2,1)}, u32[]{:S(2)}) copy-start(bf16[512,768]{0,1:T(8,128)(2,1)} %copy.94) | copy-start | bytes 2359300
  356.2 8.6 %copy-start.22 = (pred[512,512]{0,1:T(8,128)(4,1)S(1)}, pred[512,512]{0,1:T(8,128)(4,1)}, u32[]{:S(2)}) copy-start(pred[512,512]{0,1:T(8,128)(4,1)} %get-tuple-element.240) | copy-start | bytes 786436
  356.2 8.6 %copy-start.29 = (bf16[512,768]{0,1:T(8,128)(2,1)S(1)}, bf16[512,768]{0,1:T(8,128)(2,1)}, u32[]{:S(2)}) copy-start(bf16[512,768]{0,1:T(8,128)(2,1)} %copy.92) | copy-start | bytes 2359300
  356.2 8.6 %copy-start.47 = (f32[12,512]{1,0:T(8,128)S(1)}, f32[12,512]{1,0:T(8,128)}, u32[]{:S(2)}) copy-start(f32[12,512]{1,0:T(8,128)} %log_add_fusion) | copy-start | bytes 73732
  372.7 7.6 %copy-start.8 = (bf16[512,768]{0,1:T(8,128)(2,1)S(1)}, bf16[512,768]{0,1:T(8,128)(2,1)}, u32[]{:S(2)}) copy-start(bf16[512,768]{0,1:T(8,128)(2,1)} %copy.85) | copy-start | bytes 2359300
  397.1 4.6 copy-start.7
  397.1 13.0 %collective-permute-start.2 = (bf16[512,1536]{0,1:T(8,128)(2,1)}, bf16[512,1536]{0,1:T(8,128)(2,1)}, u32[]{:S(2)}, u32[]{:S(2)}) collective-permute-start(bf16[512,1536]{0,1:T(8,128)(2,1)} %pad_maximum_fusion.1), channel_id=1, source_target_pairs={{4,0},{8,4},{12,8},{16,12},{20,16},{24,20},{28,24},{5,1},{9,5},{13... | collective-permute-start | bytes 4718600 | tf_op jit(solution)/shard_map/ppermute | solution.py:17
  404.0 6.1 copy-start.15
  404.0 15.7 %slice-start.3 = ((s8[12582912]{0:T(1024)(128)(4,1)}), s8[4194304]{0:T(1024)(128)(4,1)S(1)}, s32[]{:S(2)}) async-start(s8[12582912]{0:T(1024)(128)(4,1)} %bitcast.292), calls=%async_computation.9 | async-start | bytes 8388608
  404.0 15.7 %slice-start.4 = ((s8[12582912]{0:T(1024)(128)(4,1)}), s8[4194304]{0:T(1024)(128)(4,1)S(1)}, s32[]{:S(2)}) async-start(s8[12582912]{0:T(1024)(128)(4,1)} %bitcast.292), calls=%async_computation.10 | async-start | bytes 8388608
  410.1 5.3 copy-start.4
  410.1 5.3 copy-start.27
  410.2 7.5 %copy-start.5 = (f32[12,64,512]{2,1,0:T(8,128)S(1)}, f32[12,64,512]{2,1,0:T(8,128)}, u32[]{:S(2)}) copy-start(f32[12,64,512]{2,1,0:T(8,128)} %fusion.160) | copy-start | bytes 4718596
  410.2 7.5 %copy-start.6 = (f32[12,64,512]{2,1,0:T(8,128)S(1)}, f32[12,64,512]{2,1,0:T(8,128)}, u32[]{:S(2)}) copy-start(f32[12,64,512]{2,1,0:T(8,128)} %fusion.161) | copy-start | bytes 4718596
  410.2 7.5 %copy-start.9 = (bf16[512,768]{0,1:T(8,128)(2,1)S(1)}, bf16[512,768]{0,1:T(8,128)(2,1)}, u32[]{:S(2)}) copy-start(bf16[512,768]{0,1:T(8,128)(2,1)} %copy.91) | copy-start | bytes 2359300
  413.6 6.1 slice-start.5
  413.6 24.5 %collective-permute-start.3 = (bf16[512,1536]{0,1:T(8,128)(2,1)}, bf16[512,1536]{0,1:T(8,128)(2,1)}, u32[]{:S(2)}, u32[]{:S(2)}) collective-permute-start(bf16[512,1536]{0,1:T(8,128)(2,1)} %fusion.64), channel_id=1, source_target_pairs={{4,0},{8,4},{12,8},{16,12},{20,16},{24,20},{28,24},{5,1},{9,5},{13... | collective-permute-start | bytes 4718600 | tf_op jit(solution)/shard_map/ppermute | solution.py:17
  419.8 18.4 %copy-start.14 = (f32[12,64,512]{2,1,0:T(8,128)S(1)}, f32[12,64,512]{2,1,0:T(8,128)}, u32[]{:S(2)}) copy-start(f32[12,64,512]{2,1,0:T(8,128)} %convolution_multiply_fusion) | copy-start | bytes 4718596
  423.4 17.9 %copy-start.11 = (bf16[1,512,768]{2,1,0:T(8,128)(2,1)S(1)}, bf16[1,512,768]{2,1,0:T(8,128)(2,1)}, u32[]{:S(2)}) copy-start(bf16[1,512,768]{2,1,0:T(8,128)(2,1)} %param.13) | copy-start | bytes 2359300
  423.4 17.9 %copy-start.31 = (bf16[12,64,512]{2,1,0:T(8,128)(2,1)S(1)}, bf16[12,64,512]{2,1,0:T(8,128)(2,1)}, u32[]{:S(2)}) copy-start(bf16[12,64,512]{2,1,0:T(8,128)(2,1)} %multiply_convert_fusion.4) | copy-start | bytes 2359300
  423.4 17.9 %copy-start.49 = (f32[512]{0:T(512)S(1)}, f32[512]{0:T(512)}, u32[]{:S(2)}) copy-start(f32[512]{0:T(512)} %copy-done.48) | copy-start | bytes 6148
  423.4 17.9 %copy-start.52 = (f32[512]{0:T(512)S(1)}, f32[512]{0:T(512)}, u32[]{:S(2)}) copy-start(f32[512]{0:T(512)} %copy-done.51) | copy-start | bytes 6148
  423.4 17.9 %copy-start.54 = (f32[768]{0:T(1024)S(1)}, f32[768]{0:T(1024)}, u32[]{:S(2)}) copy-start(f32[768]{0:T(1024)} %param.17) | copy-start | bytes 9220
  423.4 17.9 %copy-start.61 = (f32[768]{0:T(1024)S(1)}, f32[768]{0:T(1024)}, u32[]{:S(2)}) copy-start(f32[768]{0:T(1024)} %param.18) | copy-start | bytes 9220
  470.0 7.5 %copy-start.16 = (bf16[1,3072,768]{2,1,0:T(8,128)(2,1)S(1)}, bf16[1,3072,768]{2,1,0:T(8,128)(2,1)}, u32[]{:S(2)}) copy-start(bf16[1,3072,768]{2,1,0:T(8,128)(2,1)} %get-tuple-element.193) | copy-start | bytes 14155780
  477.5 4.5 copy-start.12
  477.5 4.5 copy-start.25
  477.5 4.5 copy-start.32
  477.5 4.5 copy-start.55
  676.4 6.6 copy-start.23
  (17 other events, 36.6 us)
Sparse Core Ops, SparseCore 0:
  313.3 156.6 all-reduce.7
  477.5 198.8 all-reduce.5
where the time goes:
time: 699 us; the launch traced here: 692 us
  waiting for transfers between devices  233 us (33%)
  matrix products  196 us (28%)
  local copies, waits for them, and re-layouts  86.4 us (12%)
  other arithmetic  74.9 us (11%)
  blocking collectives  55.8 us (8%)
  starting transfers between devices  29.9 us (4%)
  between operations  15.3 us (2%)
    psum x1, waiting for transfers between devices, on_device(): lax.psum((grad_w_qkv, grad_w_out, grad_first_gain, grad_first_bias, grad_...  129 us
    psum x1, blocking collectives, on_device(): lax.psum((grad_w_qkv, grad_w_out, grad_first_gain, grad_first_bias, grad_...  55.8 us
    dot_general x3, matrix products, step(): jnp.einsum('hqk,khd->qhd', shares.astype(jnp.bfloat16), value_rows, prefe...  34.3 us
    all_to_all x1, waiting for transfers between devices, on_device(): lax.all_to_all(send, 'exp', split_axis=0, concat_axis=0, tiled=True)  28.2 us
    dot_general x3, matrix products, step(): jnp.einsum('qhd,khd->hqk', queries, key_rows, preferred_element_type=jnp....  25.3 us
    dot_general x3, matrix products, backward_core(): jnp.einsum('qhd,khd->hqk', grad_heads, value_rows, preferred_element_type...  23.4 us
    psum x1, waiting for transfers between devices, on_device(): lax.psum(grad_w_up.astype(jnp.bfloat16), 'seq').astype(jnp.float32)  23.3 us
    all_to_all x1, waiting for transfers between devices, on_device(): lax.all_to_all(grad_slots.reshape(experts_total, capacity, width), 'exp',...  19.5 us
  transfers between devices with their start and end apart: 10, of which 7 were waited for; matrix products, arithmetic and copies ran while one was open for 36% of the time, Pallas kernels for 0%

commit v1 on v0

--- a/solution.py
+++ b/solution.py
@@ -290,15 +290,18 @@
     grad_first_bias = jnp.sum(grad_attn_in, axis=0)
     grad_input = grad_resid + norm_back(grad_attn_in * first_gain, normed_one, scale_one)
     dense = lax.psum(
-        (
-            grad_w_qkv,
-            grad_w_out,
-            grad_first_gain,
-            grad_first_bias,
-            grad_second_gain,
-            grad_second_bias,
+        lax.psum(
+            (
+                grad_w_qkv,
+                grad_w_out,
+                grad_first_gain,
+                grad_first_bias,
+                grad_second_gain,
+                grad_second_bias,
+            ),
+            "exp",
         ),
-        ("seq", "exp"),
+        "seq",
     )
     expert_sums = (
         lax.psum(grad_w_up.astype(jnp.bfloat16), "seq").astype(jnp.float32),

time: 699 us -> 1060 us (1.52)
  waiting for transfers between devices: 233 us -> 591 us
  blocking collectives: 55.8 us -> 84.3 us
  matrix products: 196 us -> 183 us
    psum x1, waiting for transfers between devices: 129 us -> 320 us  [on_device(): lax.psum((grad_w_qkv, grad_w_out, grad_first_gain, grad_first_bias, grad_...]
    psum x1, waiting for transfers between devices: 23.3 us -> 142 us  [on_device(): lax.psum(grad_w_up.astype(jnp.bfloat16), 'seq').astype(jnp.float32)]
    psum x0 -> x1, waiting for transfers between devices: none -> 77.6 us  [on_device(): lax.psum(lax.psum((grad_w_qkv, grad_w_out, grad_first_gain, grad_first_bi...]
    all_to_all x0 -> x1, blocking collectives: none -> 40.7 us  [on_device(): lax.all_to_all(send, 'exp', split_axis=0, concat_axis=0, tiled=True)]
    psum x1, blocking collectives: 55.8 us -> 19.4 us  [on_device(): lax.psum((grad_w_qkv, grad_w_out, grad_first_gain, grad_first_bias, grad_...]
    all_to_all x1 -> x0, waiting for transfers between devices: 28.2 us -> none  [on_device(): lax.all_to_all(send, 'exp', split_axis=0, concat_axis=0, tiled=True)]
    psum x0 -> x1, blocking collectives: none -> 24.3 us  [on_device(): lax.psum(lax.psum((grad_w_qkv, grad_w_out, grad_first_gain, grad_first_bi...]
    dot_general x3, matrix products: 34.3 us -> 22.4 us  [step(): jnp.einsum('hqk,khd->qhd', shares.astype(jnp.bfloat16), value_rows, prefe...]
  transfers between devices with their start and end apart: 10 -> 10, of which waited for: 7 -> 7; matrix products, arithmetic and copies ran while one was open for 36% -> 17% of each run, Pallas kernels for 0% -> 0%
where the time goes in v1:
time: 1060 us
  waiting for transfers between devices  591 us (56%)
  matrix products  183 us (17%)
  local copies, waits for them, and re-layouts  84.3 us (8%)
  blocking collectives  84.3 us (8%)
  other arithmetic  74.7 us (7%)
  starting transfers between devices  24.4 us (2%)
  between operations  14.8 us (1%)
    psum x1, waiting for transfers between devices, on_device(): lax.psum((grad_w_qkv, grad_w_out, grad_first_gain, grad_first_bias, grad_...  320 us
    psum x1, waiting for transfers between devices, on_device(): lax.psum(grad_w_up.astype(jnp.bfloat16), 'seq').astype(jnp.float32)  142 us
    psum x1, waiting for transfers between devices, on_device(): lax.psum(lax.psum((grad_w_qkv, grad_w_out, grad_first_gain, grad_first_bi...  77.6 us
    all_to_all x1, blocking collectives, on_device(): lax.all_to_all(send, 'exp', split_axis=0, concat_axis=0, tiled=True)  40.7 us
    dot_general x3, matrix products, step(): jnp.einsum('qhd,khd->hqk', queries, key_rows, preferred_element_type=jnp....  25.3 us
    psum x1, blocking collectives, on_device(): lax.psum(lax.psum((grad_w_qkv, grad_w_out, grad_first_gain, grad_first_bi...  24.3 us
    all_to_all x1, waiting for transfers between devices, on_device(): lax.all_to_all(grad_slots.reshape(experts_total, capacity, width), 'exp',...  23.4 us
    dot_general x3, matrix products, step(): jnp.einsum('hqk,khd->qhd', shares.astype(jnp.bfloat16), value_rows, prefe...  22.4 us
  transfers between devices with their start and end apart: 10, of which 7 were waited for; matrix products, arithmetic and copies ran while one was open for 17% of the time, Pallas kernels for 0%

profile of v1, /device:TPU:0, one launch (start us, length us, event | category | flops | bytes accessed | tf_op | source)
XLA Modules:
  0.0 1056.4 jit_solution(16201259911674707032)
XLA Ops:
  10.2 3.3 convolution_convert_fusion
  16.2 3.5 collective-permute-start
  19.8 3.4 gather_fusion
  23.8 3.8 sort.31
  27.7 6.9 gather_fusion.1
  35.4 3.1 fusion.155
  40.7 4.6 collective-permute-start.1
  53.5 7.0 gather_fusion.4
  60.5 8.6 select_reduce_fusion.2
  69.1 2.6 fusion.157
  76.3 8.7 select_reduce_fusion.1
  85.0 2.6 fusion.156
  92.2 8.0 select_reduce_fusion
  100.9 7.3 fusion.13
  108.2 8.9 fusion.36
  117.1 3.5 fusion.11
  120.7 4.6 fusion.38
  125.4 7.3 fusion.15
  132.8 8.8 fusion.158
  145.5 7.0 gather_fusion.2
  152.5 3.3 broadcast_select_fusion
  155.9 40.7 %all_to_all.20 = bf16[4,256,768]{2,1,0:T(8,128)(2,1)} all-to-all(bf16[4,256,768]{2,1,0:T(8,128)(2,1)S(1)} %get-tuple-element.262), channel_id=1, replica_groups=mesh['seq'=8,'exp'=4] {'exp'}, dimensions={0} | all-to-all | bytes 3145728 | tf_op jit(solution)/shard_map/all_to_all | solution.py:207
  196.6 4.3 all-to-all-start.2
  200.9 7.4 fusion.54
  208.3 4.5 copy-done.65
  212.8 10.7 %fusion.77 = bf16[4,256,768]{2,1,0:T(8,128)(2,1)} fusion(bf16[1,3072,768]{2,1,0:T(8,128)(2,1)} %param.24, f32[4,256,3072]{2,1,0:T(8,128)S(1)} %fusion.54), kind=kOutput, calls=%fused_computation.95 | convolution fusion | flops 4860936192 | bytes 18874368 | tf_op jit(solution)/shard_map/secf,efd->secd/dot_general | solution.py:212
  223.5 13.5 %all-to-all-done.2 = bf16[4,256,768]{2,1,0:T(8,128)(2,1)} async-done(((bf16[4,256,768]{2,1,0:T(8,128)(2,1)}), bf16[4,256,768]{2,1,0:T(8,128)(2,1)}, u32[]{:S(2)}, u32[]{:S(2)}) %all-to-all-start.2) | async-done | bytes 1572896 | tf_op jit(solution)/shard_map/all_to_all | solution.py:227
  237.1 4.4 all-to-all-start.1
  241.5 15.3 %fusion.6 = bf16[4,1,256,3072]{3,2,0,1:T(8,128)(2,1)S(1)} fusion(f32[4,256,3072]{2,1,0:T(8,128)} %copy-done.65, bf16[4,256,768]{2,1,0:T(8,128)(2,1)} %all-to-all-done.2, bf16[1,3072,768]{2,1,0:T(8,128)(2,1)} %param.24), kind=kOutput, calls=%fused_computation.14 | convolution fusion | flops 4894752768 | bytes 25165824 | tf_op jit(solution)/shard_map/secd,efd->secf/dot_general | solution.py:233
  256.8 2.7 copy-done.64
  259.5 8.5 fusion.82
  268.1 9.9 all-to-all-done.1
  278.0 4.4 all-to-all-start.3
  283.0 4.4 sort.32
  290.4 5.1 gather_fusion.3
  295.5 23.4 %all-to-all-done.3 = bf16[4,256,768]{2,1,0:T(8,128)(2,1)} async-done(((bf16[4,256,768]{2,1,0:T(8,128)(2,1)}), bf16[4,256,768]{2,1,0:T(8,128)(2,1)}, u32[]{:S(2)}, u32[]{:S(2)}) %all-to-all-start.3) | async-done | bytes 1572896 | tf_op jit(solution)/shard_map/all_to_all | solution.py:241
  318.9 4.7 gather_fusion.5
  323.5 3.1 fusion.102
  326.6 3.6 fusion.100
  337.3 8.3 fusion.110
  345.6 7.0 multiply_convert_fusion
  352.7 7.5 multiply_convert_fusion.2
  360.2 2.3 fusion.160
  362.5 3.1 convolution_multiply_fusion
  365.7 7.2 multiply_convert_fusion.1
  377.6 3.1 convolution_multiply_fusion.1
  380.7 2.4 fusion.161
  383.1 6.1 fusion.30
  389.2 3.6 fusion.64
  398.7 3.7 fusion.32
  402.5 4.9 collective-permute-done.3
  410.6 5.3 fusion.106
  416.2 9.1 fusion.56
  425.3 12.1 %fusion.59 = bf16[1,3072,768]{2,1,0:T(8,128)(2,1)} fusion(bf16[4,256,768]{2,1,0:T(8,128)(2,1)} %all-to-all-done.2, f32[4,256,3072]{2,1,0:T(8,128)} %copy-done.65), kind=kOutput, calls=%fused_computation.72 | convolution fusion | flops 4862509056 | bytes 18874368 | tf_op jit(solution)/shard_map/secf,secd->efd/dot_general | solution.py:230
  437.4 319.7 %all-reduce.11.cloned.1.call-done = (f32[768,2304]{1,0:T(8,128)}, f32[768,768]{1,0:T(8,128)}) async-done(((f32[768,2304]{1,0:T(8,128)}, f32[768,768]{1,0:T(8,128)}), (f32[768,2304]{1,0:T(8,128)}, f32[768,768]{1,0:T(8,128)})) %all-reduce.11.cloned.1.call-update) | async-done | bytes 9437200 | tf_op jit(solution)/shard_map/psum | solution.py:293
  757.1 141.6 %all-reduce.13.cloned.1.call-done = (bf16[1,768,3072]{2,1,0:T(8,128)(2,1)}, bf16[1,3072,768]{2,1,0:T(8,128)(2,1)}) async-done(((bf16[1,768,3072]{2,1,0:T(8,128)(2,1)}, bf16[1,3072,768]{2,1,0:T(8,128)(2,1)}), (bf16[1,768,3072]{2,1,0:T(8,128)(2,1)}, bf16[1,3072,768]{2,1,0:T(8,128)(2,1)})) %all-reduce.13.cloned.1.call-update) | async-done | bytes 9437200 | tf_op jit(solution)/shard_map/psum | solution.py:307
  898.7 7.5 convert_element_type.162
  906.2 4.9 convert_element_type.165
  911.1 4.2 fusion.96
  915.3 19.4 %all-reduce.2 = (f32[768]{0:T(1024)}, f32[768]{0:T(1024)}, f32[768]{0:T(1024)}, f32[768]{0:T(1024)}) all-reduce(f32[768]{0:T(1024)} %get-tuple-element.167, f32[768]{0:T(1024)} %get-tuple-element.170, f32[768]{0:T(1024)S(1)} %get-tuple-element.165, f32[768]{0:T(1024)S(1)} %copy-done.50), channel_id=1, replica_groups=mesh['seq'=8,'exp'=4] {'exp'}, use_global_device_ids=true, to_apply=%region_25.26 | all-reduce | flops 3072 | bytes 24576 | tf_op jit(solution)/shard_map/psum | solution.py:293
  934.6 24.3 %all-reduce = (f32[768]{0:T(1024)}, f32[768]{0:T(1024)}, f32[768]{0:T(1024)}, f32[768]{0:T(1024)}) all-reduce(f32[768]{0:T(1024)} %get-tuple-element.192, f32[768]{0:T(1024)} %get-tuple-element.193, f32[768]{0:T(1024)} %get-tuple-element.194, f32[768]{0:T(1024)} %get-tuple-element.195), channel_id=1, replica_groups=mesh['seq'=8,'exp'=4] {'seq'}, use_global_device_ids=true, to_apply=%region_26.27 | all-reduce | flops 3072 | bytes 24576 | tf_op jit(solution)/shard_map/psum | solution.py:292
  960.3 3.8 fusion.95
  964.1 77.6 %all-reduce.9.cloned.1.call-done = (f32[768,2304]{1,0:T(8,128)}, f32[768,768]{1,0:T(8,128)}) async-done(((f32[768,2304]{1,0:T(8,128)}, f32[768,768]{1,0:T(8,128)}), (f32[768,2304]{1,0:T(8,128)}, f32[768,768]{1,0:T(8,128)})) %all-reduce.9.cloned.1.call-update) | async-done | bytes 9437200 | tf_op jit(solution)/shard_map/psum | solution.py:292
  1041.6 6.6 copy.134
  (212 shorter events, 59.0 us)
Async XLA Ops:
  8.7 4.9 copy-start.48
  10.2 9.5 copy-start.57
  16.2 24.5 %collective-permute-start = (bf16[512,1536]{1,0:T(8,128)(2,1)}, bf16[512,1536]{1,0:T(8,128)(2,1)}, u32[]{:S(2)}, u32[]{:S(2)}) collective-permute-start(bf16[512,1536]{1,0:T(8,128)(2,1)} %slice.67), channel_id=1, source_target_pairs={{0,4},{4,8},{8,12},{12,16},{16,20},{20,24},{24,28},{1,5},{5,9},{9,... | collective-permute-start | bytes 4718600 | tf_op jit(solution)/shard_map/ppermute | solution.py:17
  35.4 18.1 %copy-start.44 = (s32[1024]{0:T(1024)}, s32[1024]{0:T(1024)S(1)}, u32[]{:S(2)}) copy-start(s32[1024]{0:T(1024)S(1)} %broadcast_clamp_fusion) | copy-start | bytes 12292
  40.7 44.3 %collective-permute-start.1 = (bf16[512,1536]{1,0:T(8,128)(2,1)}, bf16[512,1536]{1,0:T(8,128)(2,1)}, u32[]{:S(2)}, u32[]{:S(2)}) collective-permute-start(bf16[512,1536]{1,0:T(8,128)(2,1)} %collective-permute-done), channel_id=1, source_target_pairs={{0,4},{4,8},{8,12},{12,16},{16,20},{20,24},{24,28},{1,5},{5,9},{9,... | collective-permute-start | bytes 4718600 | tf_op jit(solution)/shard_map/ppermute | solution.py:17
  92.2 8.0 copy-start.33
  92.2 8.0 copy-start.39
  92.2 8.6 copy-start.19
  100.2 7.9 copy-start.41
  100.8 7.3 copy-start.38
  100.8 16.3 %slice-start = ((s8[12582912]{0:T(1024)(128)(4,1)}), s8[4194304]{0:T(1024)(128)(4,1)S(1)}, s32[]{:S(2)}) async-start(s8[12582912]{0:T(1024)(128)(4,1)} %bitcast.290), calls=%async_computation.7 | async-start | bytes 8388608
  100.8 16.3 %slice-start.1 = ((s8[12582912]{0:T(1024)(128)(4,1)}), s8[4194304]{0:T(1024)(128)(4,1)S(1)}, s32[]{:S(2)}) async-start(s8[12582912]{0:T(1024)(128)(4,1)} %bitcast.290), calls=%async_computation.8 | async-start | bytes 8388608
  108.2 24.5 %copy-start.34 = (f32[12,512]{1,0:T(8,128)}, f32[12,512]{1,0:T(8,128)S(1)}, u32[]{:S(2)}) copy-start(f32[12,512]{1,0:T(8,128)S(1)} %fusion.13) | copy-start | bytes 73732
  108.2 9.0 slice-start.2
  120.7 12.0 %copy-start.35 = (f32[12,512]{1,0:T(8,128)}, f32[12,512]{1,0:T(8,128)S(1)}, u32[]{:S(2)}) copy-start(f32[12,512]{1,0:T(8,128)S(1)} %fusion.11) | copy-start | bytes 73732
  125.3 7.4 copy-start.40
  125.3 7.4 copy-start.42
  125.3 7.4 copy-start.21
  125.3 7.4 copy-start.28
  125.3 7.4 copy-start.37
  125.4 7.4 copy-start.62
  125.4 7.4 copy-start.63
  132.7 8.9 copy-start.36
  132.8 8.8 copy-start.10
  132.8 8.8 copy-start.59
  196.6 40.5 %all-to-all-start.2 = ((bf16[4,256,768]{2,1,0:T(8,128)(2,1)}), bf16[4,256,768]{2,1,0:T(8,128)(2,1)}, u32[]{:S(2)}, u32[]{:S(2)}) async-start(bf16[4,256,768]{2,1,0:T(8,128)(2,1)} %get-tuple-element.248), calls=%async_computation.2 | async-start | bytes 3145728 | tf_op jit(solution)/shard_map/all_to_all | solution.py:227
  208.3 4.5 copy-start.65
  237.1 40.9 %all-to-all-start.1 = ((bf16[4,256,768]{2,1,0:T(8,128)(2,1)}), bf16[4,256,768]{2,1,0:T(8,128)(2,1)}, u32[]{:S(2)}, u32[]{:S(2)}) async-start(bf16[4,256,768]{2,1,0:T(8,128)(2,1)} %fusion.77), calls=%async_computation.1 | async-start | bytes 3145728 | tf_op jit(solution)/shard_map/all_to_all | solution.py:215
  278.0 40.9 %all-to-all-start.3 = ((bf16[4,256,768]{2,1,0:T(8,128)(2,1)}), bf16[4,256,768]{2,1,0:T(8,128)(2,1)}, u32[]{:S(2)}, u32[]{:S(2)}) async-start(bf16[4,256,768]{2,1,0:T(8,128)(2,1)} %fusion.82), calls=%async_computation.3 | async-start | bytes 3145728 | tf_op jit(solution)/shard_map/all_to_all | solution.py:241
  282.3 474.7 %all-reduce.11.cloned.1.call-start = ((), (), s32[]{:S(2)}) async-start(), calls=%async_computation.5 | async-start | bytes 18874368 | tf_op jit(solution)/shard_map/psum | solution.py:293
  295.5 28.1 %copy-start.46 = (f32[512]{0:T(512)S(1)}, f32[512]{0:T(512)}, u32[]{:S(2)}) copy-start(f32[512]{0:T(512)} %copy-done.45) | copy-start | bytes 6148
  323.5 7.8 copy-start.60
  337.3 8.3 copy-start.17
  337.3 8.3 copy-start.22
  337.3 8.3 copy-start.29
  337.3 8.3 copy-start.47
  352.7 7.5 copy-start.8
  376.1 4.6 copy-start.7
  376.1 13.1 %collective-permute-start.2 = (bf16[512,1536]{0,1:T(8,128)(2,1)}, bf16[512,1536]{0,1:T(8,128)(2,1)}, u32[]{:S(2)}, u32[]{:S(2)}) collective-permute-start(bf16[512,1536]{0,1:T(8,128)(2,1)} %pad_maximum_fusion.1), channel_id=1, source_target_pairs={{4,0},{8,4},{12,8},{16,12},{20,16},{24,20},{28,24},{5,1},{9,5},{13... | collective-permute-start | bytes 4718600 | tf_op jit(solution)/shard_map/ppermute | solution.py:17
  383.1 6.1 copy-start.15
  383.1 15.6 %slice-start.3 = ((s8[12582912]{0:T(1024)(128)(4,1)}), s8[4194304]{0:T(1024)(128)(4,1)S(1)}, s32[]{:S(2)}) async-start(s8[12582912]{0:T(1024)(128)(4,1)} %bitcast.292), calls=%async_computation.10 | async-start | bytes 8388608
  383.1 15.6 %slice-start.4 = ((s8[12582912]{0:T(1024)(128)(4,1)}), s8[4194304]{0:T(1024)(128)(4,1)S(1)}, s32[]{:S(2)}) async-start(s8[12582912]{0:T(1024)(128)(4,1)} %bitcast.292), calls=%async_computation.11 | async-start | bytes 8388608
  389.2 5.2 copy-start.4
  389.2 5.2 copy-start.27
  389.2 7.4 copy-start.5
  389.2 7.4 copy-start.6
  389.2 7.3 copy-start.9
  392.8 5.9 slice-start.5
  392.8 14.5 %collective-permute-start.3 = (bf16[512,1536]{0,1:T(8,128)(2,1)}, bf16[512,1536]{0,1:T(8,128)(2,1)}, u32[]{:S(2)}, u32[]{:S(2)}) collective-permute-start(bf16[512,1536]{0,1:T(8,128)(2,1)} %fusion.64), channel_id=1, source_target_pairs={{4,0},{8,4},{12,8},{16,12},{20,16},{24,20},{28,24},{5,1},{9,5},{13... | collective-permute-start | bytes 4718600 | tf_op jit(solution)/shard_map/ppermute | solution.py:17
  398.7 8.7 copy-start.14
  402.4 8.1 copy-start.11
  402.4 8.1 copy-start.31
  402.5 8.1 copy-start.49
  402.5 8.1 copy-start.52
  402.5 8.1 copy-start.54
  402.5 8.1 copy-start.61
  415.9 482.7 %all-reduce.13.cloned.1.call-start = ((), (), s32[]{:S(2)}) async-start(), calls=%async_computation.6 | async-start | bytes 18874368 | tf_op jit(solution)/shard_map/psum | solution.py:307
  437.4 604.3 %all-reduce.9.cloned.1.call-start = ((), (), s32[]{:S(2)}) async-start(), calls=%async_computation.4 | async-start | bytes 18874368 | tf_op jit(solution)/shard_map/psum | solution.py:292
  898.7 7.5 copy-start.16
  906.2 4.9 copy-start.12
  906.2 4.9 copy-start.25
  906.2 4.9 copy-start.32
  906.2 4.9 copy-start.55
  1041.6 6.6 copy-start.23
  (18 other events, 39.2 us)
Sparse Core Ops, SparseCore 0:
  416.1 340.9 all-reduce.10
  761.4 137.2 all-reduce.12
  902.9 138.7 all-reduce.8
